TPU v7x, 32 devices: a whole 2x2x4 slice. The times are simulated.
32 devices in a mesh: dp: 8 (over y, x, core), head: 4 (over z).
Axes of the slice: x: 2, y: 2, z: 4, core: 2. Of those that a mesh axis runs over, the one named last changes fastest.
Arguments:
- stream: float32 [8192, 1024], P(('dp', 'head')), may hold values from -16 to 16
- cotangent: float32 [8192, 1024], P(('dp', 'head')), may hold values from -16 to 16
- documents: int32 [8, 1024], P('dp'), may hold values from 0 to 3, never falling along the last dimension, each value on 1 to 512 neighbouring positions
- attend_weight: bfloat16 [2, 3, 1024, 1024], P(None, None, None, 'head'), may hold values from -0.1875 to 0.1875
- output_weight: bfloat16 [2, 1024, 1024], P(None, 'head'), may hold values from -0.1875 to 0.1875
- expand_weight: bfloat16 [2, 2, 1024, 4096], P(None, None, None, 'head'), may hold values from -0.1875 to 0.1875
- reduce_weight: bfloat16 [2, 4096, 1024], P(None, 'head'), may hold values from -0.09375 to 0.09375
- score_gain: float32 [2, 1024], P(None, 'head'), may hold values from 0.8 to 1.6
- unit_gain: float32 [2, 2, 4096], P(None, None, 'head'), may hold values from 0.5 to 2
- alphas: float32 [2, 2, 1024], replicated, may hold values from 0.1 to 0.5
Outputs:
- result: float32 [8192, 1024], P(('dp', 'head'))
- stream_delta: float32 [8192, 1024], P(('dp', 'head'))
- attend_delta: float32 [2, 3, 1024, 1024], P(None, None, 'dp', 'head')
- output_delta: float32 [2, 1024, 1024], P(None, 'head', 'dp')
- expand_delta: float32 [2, 2, 1024, 4096], P(None, None, 'dp', 'head')
- reduce_delta: float32 [2, 4096, 1024], P(None, 'head', 'dp')
- score_delta: float32 [2, 1024], P(None, 'head')
- unit_delta: float32 [2, 2, 4096], P(None, None, 'head')
- alpha_delta: float32 [2, 2, 1024], replicated
- total_norm: float32 [], replicated
- alpha_mean: float32 [2, 2], replicated
Inputs may be any that keep to these rules, and one draw needn't show every extreme that they name: `documents`: document numbers never fall along a sequence; a document holds at most 512 positions.
All inputs are finite; a program needn't handle non-finite values.
Results may differ from a plain program's by a relative error of at most 0.034.
Values may be sent and summed in bfloat16 or wider, within the bound.
No kernel may reach another device: no remote copies, remote signals or barrier semaphores. Data moves between devices by JAX's collectives and lax.ppermute only.
A program may use at most 256 MiB of HBM per device.

v0:
```python
import jax
import jax.numpy as jnp
from jax import lax
from jax.sharding import PartitionSpec as P

D = 1024
HDIM = 64


def sphere(values):
    return values * lax.rsqrt(jnp.sum(values * values, axis=-1, keepdims=True) + 1e-06)


def blend_unit(hidden, branch, mixing):
    return sphere(hidden + mixing * (sphere(branch) - hidden))


def gated_units(up_part, gate_part, up_gain, gate_gain):
    return up_part * up_gain * jax.nn.silu(gate_part * gate_gain * D**0.5)


def unit_heads(values, scales):
    heads_here = values.shape[1] // HDIM
    split = values.reshape(values.shape[0], heads_here, HDIM)
    return (sphere(split) * scales.reshape(heads_here, HDIM)).reshape(values.shape)


def spread_rows(local_values):
    return lax.all_gather(local_values, "head", axis=0, tiled=True)


def spread_grads(local_values):
    return lax.all_gather(local_values, "head", axis=0, tiled=True)


def collect_rows(source, weight, local_rows):

    def partial_term(first_row, row_count):
        return jnp.dot(source, weight, preferred_element_type=jnp.float32)

    return lax.psum_scatter(
        partial_term(jnp.int32(0), local_rows * lax.axis_size("head")).astype(jnp.bfloat16),
        "head",
        scatter_dimension=0,
        tiled=True,
    ).astype(jnp.float32)


def branch_output(context, weight, local_rows):

    def partial_term(first_row, row_count):
        return jnp.dot(context, weight, preferred_element_type=jnp.float32)

    return lax.psum_scatter(
        partial_term(jnp.int32(0), local_rows * lax.axis_size("head")),
        "head",
        scatter_dimension=0,
        tiled=True,
    )


def collect_grads(products, local_rows):

    def partial_term(first_row, row_count):
        summed_terms = None
        for grad_rows, weight in products:
            entry = lax.dot_general(
                grad_rows, weight, (((1,), (1,)), ((), ())), preferred_element_type=jnp.float32
            )
            summed_terms = entry if summed_terms is None else summed_terms + entry
        return summed_terms

    return lax.psum_scatter(
        partial_term(jnp.int32(0), local_rows * lax.axis_size("head")).astype(jnp.bfloat16),
        "head",
        scatter_dimension=0,
        tiled=True,
    ).astype(jnp.float32)


def visible(labels):
    positions = jnp.arange(labels.shape[0])
    return (positions[:, None] >= positions[None, :]) & (labels[:, None] == labels[None, :])


def by_sequence(values, documents):
    heads_here = values.shape[1] // HDIM
    return values.reshape(documents.shape[0], documents.shape[1], heads_here, HDIM)


def attend_forward(query_unit, key_unit, value_rows, documents):

    def per_sequence(inputs):
        queries, key_rows, values, labels = inputs
        logits = HDIM**0.5 * jnp.einsum(
            "qhd,khd->hqk", queries, key_rows, preferred_element_type=jnp.float32
        )
        scores = jnp.where(visible(labels)[None], logits, -1e30)
        peaks = jnp.max(scores, axis=-1, keepdims=True)
        powers = jnp.exp(scores - peaks)
        totals = jnp.sum(powers, axis=-1, keepdims=True)
        weights = (powers / totals).astype(jnp.bfloat16)
        context = jnp.einsum("hqk,khd->qhd", weights, values, preferred_element_type=jnp.float32)
        return (context.astype(jnp.bfloat16), (peaks + jnp.log(totals))[..., 0])

    context, logsum = lax.map(
        per_sequence,
        (
            by_sequence(query_unit, documents),
            by_sequence(key_unit, documents),
            by_sequence(value_rows, documents),
            documents,
        ),
    )
    return (context.reshape(query_unit.shape), logsum)


def attend_backward(query_unit, key_unit, value_rows, documents, logsum, context_grad):

    def per_sequence(inputs):
        queries, key_rows, values, labels, lse_rows, grads = inputs
        logits = HDIM**0.5 * jnp.einsum(
            "qhd,khd->hqk", queries, key_rows, preferred_element_type=jnp.float32
        )
        scores = jnp.where(visible(labels)[None], logits, -1e30)
        probs = jnp.exp(scores - lse_rows[..., None])
        prob_grad = jnp.einsum("qhd,khd->hqk", grads, values, preferred_element_type=jnp.float32)
        inner = jnp.sum(probs * prob_grad, axis=-1, keepdims=True)
        logit_grad = (probs * (prob_grad - inner)).astype(jnp.bfloat16)
        query_grad = HDIM**0.5 * jnp.einsum(
            "hqk,khd->qhd", logit_grad, key_rows, preferred_element_type=jnp.float32
        )
        key_grad = HDIM**0.5 * jnp.einsum(
            "hqk,qhd->khd", logit_grad, queries, preferred_element_type=jnp.float32
        )
        value_grad = jnp.einsum(
            "hqk,qhd->khd", probs.astype(jnp.bfloat16), grads, preferred_element_type=jnp.float32
        )
        return (query_grad, key_grad, value_grad)

    query_grad, key_grad, value_grad = lax.map(
        per_sequence,
        (
            by_sequence(query_unit, documents),
            by_sequence(key_unit, documents),
            by_sequence(value_rows, documents),
            documents,
            logsum,
            by_sequence(context_grad, documents),
        ),
    )
    return (
        query_grad.reshape(query_unit.shape),
        key_grad.reshape(query_unit.shape),
        value_grad.reshape(query_unit.shape),
    )


def rows_product(rows_low, grads_low):
    return lax.dot_general(
        rows_low, grads_low, (((0,), (0,)), ((), ())), preferred_element_type=jnp.float32
    )


def on_device(
    stream,
    cotangent,
    documents,
    attend_weight,
    output_weight,
    expand_weight,
    reduce_weight,
    score_gain,
    unit_gain,
    alphas,
):
    local_rows = stream.shape[0]
    depth = attend_weight.shape[0]
    hidden = sphere(stream)
    records = []
    for layer_index in range(depth):
        weights_in = attend_weight[layer_index]
        hidden_low = hidden.astype(jnp.bfloat16)
        attend_rows = spread_rows(hidden_low)
        queries = jnp.dot(attend_rows, weights_in[0], preferred_element_type=jnp.float32)
        key_rows = jnp.dot(attend_rows, weights_in[1], preferred_element_type=jnp.float32)
        value_rows = jnp.dot(attend_rows, weights_in[2], preferred_element_type=jnp.float32).astype(
            jnp.bfloat16
        )
        query_unit = unit_heads(queries, score_gain[layer_index]).astype(jnp.bfloat16)
        key_unit = unit_heads(key_rows, score_gain[layer_index]).astype(jnp.bfloat16)
        context, logsum = attend_forward(query_unit, key_unit, value_rows, documents)
        branch = branch_output(context, output_weight[layer_index], local_rows)
        middle = blend_unit(hidden, branch, alphas[layer_index, 0])
        middle_low = middle.astype(jnp.bfloat16)
        expand_rows = spread_rows(middle_low)
        up_part = jnp.dot(
            expand_rows, expand_weight[layer_index, 0], preferred_element_type=jnp.float32
        )
        gate_part = jnp.dot(
            expand_rows, expand_weight[layer_index, 1], preferred_element_type=jnp.float32
        )
        units = gated_units(
            up_part, gate_part, unit_gain[layer_index, 0], unit_gain[layer_index, 1]
        ).astype(jnp.bfloat16)
        reduced = collect_rows(units, reduce_weight[layer_index], local_rows)
        kept_rows = (attend_rows, expand_rows)
        records.append(
            (
                hidden,
                middle,
                branch,
                reduced,
                kept_rows,
                queries,
                key_rows,
                query_unit,
                key_unit,
                value_rows,
                context,
                logsum,
                up_part,
                gate_part,
                units,
            )
        )
        hidden = blend_unit(middle, reduced, alphas[layer_index, 1])
    flowing = cotangent
    weight_parts = [None] * depth
    score_parts = [None] * depth
    unit_parts = [None] * depth
    alpha_parts = [None] * depth
    for layer_index in range(depth - 1, -1, -1):
        (
            before,
            middle,
            branch,
            reduced,
            kept_rows,
            queries,
            key_rows,
            query_unit,
            key_unit,
            value_rows,
            context,
            logsum,
            up_part,
            gate_part,
            units,
        ) = records[layer_index]
        attend_rows = kept_rows[0]
        expand_rows = kept_rows[1]
        unused, pullback = jax.vjp(blend_unit, middle, reduced, alphas[layer_index, 1])
        middle_grad, reduced_grad, alpha_second = pullback(flowing)
        reduced_full = spread_grads(reduced_grad.astype(jnp.bfloat16))
        units_grad = lax.dot_general(
            reduced_full,
            reduce_weight[layer_index],
            (((1,), (1,)), ((), ())),
            preferred_element_type=jnp.float32,
        )
        reduce_part = rows_product(units, reduced_full)
        unused, pull_gate = jax.vjp(
            gated_units, up_part, gate_part, unit_gain[layer_index, 0], unit_gain[layer_index, 1]
        )
        up_grad, gate_grad, up_gain_grad, gate_gain_grad = pull_gate(units_grad)
        up_low = up_grad.astype(jnp.bfloat16)
        gate_low = gate_grad.astype(jnp.bfloat16)
        expand_part = jnp.stack(
            [rows_product(expand_rows, up_low), rows_product(expand_rows, gate_low)]
        )
        middle_grad = middle_grad + collect_grads(
            ((up_low, expand_weight[layer_index, 0]), (gate_low, expand_weight[layer_index, 1])),
            local_rows,
        )
        unused, pullback = jax.vjp(blend_unit, before, branch, alphas[layer_index, 0])
        hidden_grad, branch_grad, alpha_first = pullback(middle_grad)
        branch_full = spread_grads(branch_grad.astype(jnp.bfloat16))
        context_grad = lax.dot_general(
            branch_full,
            output_weight[layer_index],
            (((1,), (1,)), ((), ())),
            preferred_element_type=jnp.float32,
        ).astype(jnp.bfloat16)
        output_part = rows_product(context, branch_full)
        query_unit_grad, key_unit_grad, value_grad = attend_backward(
            query_unit, key_unit, value_rows, documents, logsum, context_grad
        )
        unused, pull_query = jax.vjp(unit_heads, queries, score_gain[layer_index])
        query_grad, query_gain = pull_query(query_unit_grad)
        unused, pull_key = jax.vjp(unit_heads, key_rows, score_gain[layer_index])
        key_grad, key_gain = pull_key(key_unit_grad)
        query_low = query_grad.astype(jnp.bfloat16)
        key_low = key_grad.astype(jnp.bfloat16)
        value_low = value_grad.astype(jnp.bfloat16)
        attend_part = jnp.stack(
            [
                rows_product(attend_rows, query_low),
                rows_product(attend_rows, key_low),
                rows_product(attend_rows, value_low),
            ]
        )
        weights_in = attend_weight[layer_index]
        flowing = hidden_grad + collect_grads(
            ((query_low, weights_in[0]), (key_low, weights_in[1]), (value_low, weights_in[2])),
            local_rows,
        )
        weight_parts[layer_index] = (attend_part, output_part, expand_part, reduce_part)
        score_parts[layer_index] = query_gain + key_gain
        unit_parts[layer_index] = jnp.stack([up_gain_grad, gate_gain_grad])
        alpha_parts[layer_index] = jnp.stack([alpha_first, alpha_second])
    unused, pullback = jax.vjp(sphere, stream)
    stream_delta = pullback(flowing)[0]
    attend_stack = jnp.stack([weight_parts[index_layer][0] for index_layer in range(depth)])
    output_stack = jnp.stack([weight_parts[index_layer][1] for index_layer in range(depth)])
    expand_stack = jnp.stack([weight_parts[index_layer][2] for index_layer in range(depth)])
    reduce_stack = jnp.stack([weight_parts[index_layer][3] for index_layer in range(depth)])
    attend_delta, output_delta, expand_delta, reduce_delta = (
        lax.psum_scatter(
            attend_stack.astype(jnp.bfloat16), "dp", scatter_dimension=2, tiled=True
        ).astype(jnp.float32),
        lax.psum_scatter(
            output_stack.astype(jnp.bfloat16), "dp", scatter_dimension=2, tiled=True
        ).astype(jnp.float32),
        lax.psum_scatter(
            expand_stack.astype(jnp.bfloat16), "dp", scatter_dimension=2, tiled=True
        ).astype(jnp.float32),
        lax.psum_scatter(
            reduce_stack.astype(jnp.bfloat16), "dp", scatter_dimension=2, tiled=True
        ).astype(jnp.float32),
    )
    score_delta, unit_delta = lax.psum((jnp.stack(score_parts), jnp.stack(unit_parts)), "dp")
    alpha_delta = lax.psum(jnp.stack(alpha_parts), ("dp", "head"))
    squares = jnp.sum(attend_delta * attend_delta) + jnp.sum(output_delta * output_delta)
    squares = squares + jnp.sum(expand_delta * expand_delta) + jnp.sum(reduce_delta * reduce_delta)
    squares = squares + (
        jnp.sum(score_delta * score_delta) + jnp.sum(unit_delta * unit_delta)
    ) / lax.axis_size("dp")
    squares = squares + jnp.sum(alpha_delta * alpha_delta) / (
        lax.axis_size("dp") * lax.axis_size("head")
    )
    total_norm = jnp.sqrt(lax.psum(squares, ("dp", "head")))
    alpha_mean = jnp.mean(alphas, axis=-1)
    return (
        hidden,
        stream_delta,
        attend_delta,
        output_delta,
        expand_delta,
        reduce_delta,
        score_delta,
        unit_delta,
        alpha_delta,
        total_norm,
        alpha_mean,
    )


def solution(mesh):
    return jax.shard_map(
        on_device,
        mesh=mesh,
        in_specs=(
            P(("dp", "head"), None),
            P(("dp", "head"), None),
            P("dp", None),
            P(None, None, None, "head"),
            P(None, "head", None),
            P(None, None, None, "head"),
            P(None, "head", None),
            P(None, "head"),
            P(None, None, "head"),
            P(),
        ),
        out_specs=(
            P(("dp", "head"), None),
            P(("dp", "head"), None),
            P(None, None, "dp", "head"),
            P(None, "head", "dp"),
            P(None, None, "dp", "head"),
            P(None, "head", "dp"),
            P(None, "head"),
            P(None, None, "head"),
            P(),
            P(),
            P(),
        ),
        check_vma=False,
    )
```

profile of v0, /device:TPU:0, one launch (start us, length us, event | category | flops | bytes accessed | tf_op | source)
XLA Modules:
  0.0 1292.2 jit_solution(4551727930264226601)
XLA Ops:
  16.4 43.2 %all-gather.9.cloned.1.call-done = bf16[1024,1024]{1,0:T(8,128)(2,1)} async-done(((bf16[256,1024]{1,0:T(8,128)(2,1)}), bf16[1024,1024]{1,0:T(8,128)(2,1)}) %all-gather.9.cloned.1.call-update) | async-done | bytes 2097168 | tf_op jit(solution)/shard_map/all_gather | solution.py:29
  92.3 75.0 %reduce-scatter.17.cloned.1.call-done = f32[256,1024]{1,0:T(8,128)} async-done(((f32[1024,1024]{1,0:T(8,128)}), f32[256,1024]{1,0:T(8,128)}) %reduce-scatter.17.cloned.1.call-update) | async-done | bytes 1048592 | tf_op jit(solution)/shard_map/reduce_scatter | solution.py:54
  172.4 46.0 %all-gather.11.cloned.1.call-done = bf16[1024,1024]{1,0:T(8,128)(2,1)} async-done(((bf16[256,1024]{1,0:T(8,128)(2,1)}), bf16[1024,1024]{1,0:T(8,128)(2,1)}) %all-gather.11.cloned.1.call-update) | async-done | bytes 2097168 | tf_op jit(solution)/shard_map/all_gather | solution.py:29
  236.4 42.5 %reduce-scatter.19.cloned.1.call-done = bf16[256,1024]{1,0:T(8,128)(2,1)} async-done(((bf16[1024,1024]{1,0:T(8,128)(2,1)}), bf16[256,1024]{1,0:T(8,128)(2,1)}) %reduce-scatter.19.cloned.1.call-update) | async-done | bytes 524304 | tf_op jit(solution)/shard_map/reduce_scatter | solution.py:41
  283.4 44.2 %all-gather.13.cloned.1.call-done = bf16[1024,1024]{1,0:T(8,128)(2,1)} async-done(((bf16[256,1024]{1,0:T(8,128)(2,1)}), bf16[1024,1024]{1,0:T(8,128)(2,1)}) %all-gather.13.cloned.1.call-update) | async-done | bytes 2097168 | tf_op jit(solution)/shard_map/all_gather | solution.py:29
  359.7 75.7 %reduce-scatter.21.cloned.1.call-done = f32[256,1024]{1,0:T(8,128)} async-done(((f32[1024,1024]{1,0:T(8,128)}), f32[256,1024]{1,0:T(8,128)}) %reduce-scatter.21.cloned.1.call-update) | async-done | bytes 1048592 | tf_op jit(solution)/shard_map/reduce_scatter | solution.py:54
  439.7 46.0 %all-gather.15.cloned.1.call-done = bf16[1024,1024]{1,0:T(8,128)(2,1)} async-done(((bf16[256,1024]{1,0:T(8,128)(2,1)}), bf16[1024,1024]{1,0:T(8,128)(2,1)}) %all-gather.15.cloned.1.call-update) | async-done | bytes 2097168 | tf_op jit(solution)/shard_map/all_gather | solution.py:29
  503.7 42.5 %reduce-scatter.23.cloned.1.call-done = bf16[256,1024]{1,0:T(8,128)(2,1)} async-done(((bf16[1024,1024]{1,0:T(8,128)(2,1)}), bf16[256,1024]{1,0:T(8,128)(2,1)}) %reduce-scatter.23.cloned.1.call-update) | async-done | bytes 524304 | tf_op jit(solution)/shard_map/reduce_scatter | solution.py:41
  552.2 44.5 %all-gather.17.cloned.1.call-done = bf16[1024,1024]{1,0:T(8,128)(2,1)} async-done(((bf16[256,1024]{1,0:T(8,128)(2,1)}), bf16[1024,1024]{1,0:T(8,128)(2,1)}) %all-gather.17.cloned.1.call-update) | async-done | bytes 2097168 | tf_op jit(solution)/shard_map/all_gather | solution.py:33
  617.4 42.5 %reduce-scatter.25.cloned.1.call-done = bf16[256,1024]{1,0:T(8,128)(2,1)} async-done(((bf16[1024,1024]{1,0:T(8,128)(2,1)}), bf16[256,1024]{1,0:T(8,128)(2,1)}) %reduce-scatter.25.cloned.1.call-update) | async-done | bytes 524304 | tf_op jit(solution)/shard_map/reduce_scatter | solution.py:73
  666.8 44.8 %all-gather.19.cloned.1.call-done = bf16[1024,1024]{1,0:T(8,128)(2,1)} async-done(((bf16[256,1024]{1,0:T(8,128)(2,1)}), bf16[1024,1024]{1,0:T(8,128)(2,1)}) %all-gather.19.cloned.1.call-update) | async-done | bytes 2097168 | tf_op jit(solution)/shard_map/all_gather | solution.py:33
  724.3 15.1 %multiply_reduce_fusion.1 = (f32[4,1024]{1,0:T(4,128)S(1)}, f32[4,1024,1024]{1,2,0:T(8,128)}) fusion(f32[4,1024,1024]{1,2,0:T(8,128)} %get-tuple-element.196, f32[4,1024]{1,0:T(4,128)S(1)} %log_add_fusion.1, bf16[1024,4,64]{0,2,1:T(8,128)(2,1)} %bitcast.320, bf16[1024,4,64]{0,2,1:T(8,128)(2,1)} %bitcast.341), kind=kOutput, calls=%fused_computation.4 | convolution fusion | flops 549449728 | bytes 34635776 | tf_op jit(solution)/shard_map/while/body/eval_jaxpr/qhd,khd->hqk/dot_general | solution.py:127
  739.4 10.8 multiply_convert_fusion.1
  765.3 42.5 %reduce-scatter.27.cloned.1.call-done = bf16[256,1024]{1,0:T(8,128)(2,1)} async-done(((bf16[1024,1024]{1,0:T(8,128)(2,1)}), bf16[256,1024]{1,0:T(8,128)(2,1)}) %reduce-scatter.27.cloned.1.call-update) | async-done | bytes 524304 | tf_op jit(solution)/shard_map/reduce_scatter | solution.py:73
  813.9 44.9 %all-gather.21.cloned.1.call-done = bf16[1024,1024]{1,0:T(8,128)(2,1)} async-done(((bf16[256,1024]{1,0:T(8,128)(2,1)}), bf16[1024,1024]{1,0:T(8,128)(2,1)}) %all-gather.21.cloned.1.call-update) | async-done | bytes 2097168 | tf_op jit(solution)/shard_map/all_gather | solution.py:33
  879.9 42.5 %reduce-scatter.29.cloned.1.call-done = bf16[256,1024]{1,0:T(8,128)(2,1)} async-done(((bf16[1024,1024]{1,0:T(8,128)(2,1)}), bf16[256,1024]{1,0:T(8,128)(2,1)}) %reduce-scatter.29.cloned.1.call-update) | async-done | bytes 524304 | tf_op jit(solution)/shard_map/reduce_scatter | solution.py:73
  939.7 11.3 copy.55
  960.0 14.0 %all-gather.23.cloned.1.call-done = bf16[1024,1024]{1,0:T(8,128)(2,1)} async-done(((bf16[256,1024]{1,0:T(8,128)(2,1)}), bf16[1024,1024]{1,0:T(8,128)(2,1)}) %all-gather.23.cloned.1.call-update) | async-done | bytes 2097168 | tf_op jit(solution)/shard_map/all_gather | solution.py:33
  983.5 16.0 %multiply_reduce_fusion = (f32[4,1024]{1,0:T(4,128)}, f32[4,1024,1024]{1,2,0:T(8,128)}) fusion(f32[4,1024,1024]{1,2,0:T(8,128)} %get-tuple-element.188, f32[4,1024]{1,0:T(4,128)S(1)} %log_add_fusion, bf16[1024,4,64]{0,2,1:T(8,128)(2,1)S(1)} %bitcast.317, bf16[1024,4,64]{0,2,1:T(8,128)(2,1)S(1)} %bitcast.339), kind=kOutput, calls=%fused_computation.1 | convolution fusion | flops 549449728 | bytes 34635776 | tf_op jit(solution)/shard_map/while/body/eval_jaxpr/qhd,khd->hqk/dot_general | solution.py:127
  1001.5 10.8 multiply_convert_fusion
  1083.8 25.6 %all-reduce = (f32[2,256]{1,0:T(2,128)S(1)}, f32[2,2,1024]{2,1,0:T(2,128)S(1)}) all-reduce(f32[2,256]{1,0:T(2,128)S(1)} %pad_maximum_fusion.6, f32[2,2,1024]{2,1,0:T(2,128)S(1)} %pad_maximum_fusion.4), channel_id=1, replica_groups=mesh['dp'=8,'head'=4] {'dp'}, use_global_device_ids=true, to_apply=%region_48.49 | all-reduce | flops 4608 | bytes 36864 | tf_op jit(solution)/shard_map/psum | solution.py:332
  1116.4 37.9 %psum.30 = f32[2,2,1024]{2,1,0:T(2,128)S(1)} all-reduce(f32[2,2,1024]{2,1,0:T(2,128)S(1)} %pad_maximum_fusion.5), channel_id=1, replica_groups=mesh['dp'=8,'head'=4] {'dp','head'}, use_global_device_ids=true, to_apply=%region_58.59 | all-reduce | flops 4096 | bytes 32768 | tf_op jit(solution)/shard_map/psum | solution.py:333
  1165.4 70.9 %reduce-scatter.35.cloned.1.call-done = bf16[2,2,128,1024]{3,2,1,0:T(8,128)(2,1)} async-done(((bf16[2,2,1024,1024]{3,2,1,0:T(8,128)(2,1)}), bf16[2,2,128,1024]{3,2,1,0:T(8,128)(2,1)}) %reduce-scatter.35.cloned.1.call-update) | async-done | bytes 1048592 | tf_op jit(solution)/shard_map/reduce_scatter | solution.py:325
  1243.8 39.2 %psum.31 = f32[]{:T(128)} all-reduce(f32[]{:T(128)S(6)} %add.343), channel_id=1, replica_groups=mesh['dp'=8,'head'=4] {'dp','head'}, use_global_device_ids=true, to_apply=%region_66.67 | all-reduce | flops 1 | bytes 8 | tf_op jit(solution)/shard_map/psum | solution.py:342
  (486 shorter events, 340.5 us)
Async XLA Ops:
  7.2 52.3 %all-gather.9.cloned.1.call-start = ((), (), s32[]{:S(2)}) async-start(), calls=%async_computation.12 | async-start | bytes 2621440 | tf_op jit(solution)/shard_map/all_gather | solution.py:29
  8.8 160.5 %copy-start.78 = (f32[256]{0:T(256)}, f32[256]{0:T(256)S(1)}, u32[]{:S(2)}) copy-start(f32[256]{0:T(256)S(1)} %add_rsqrt_fusion.12) | copy-start | bytes 3076
  11.0 156.4 %reduce-scatter.17.cloned.1.call-start = ((), (), s32[]{:S(2)}) async-start(), calls=%async_computation.13 | async-start | bytes 5242880 | tf_op jit(solution)/shard_map/reduce_scatter | solution.py:54
  91.6 126.9 %all-gather.11.cloned.1.call-start = ((), (), s32[]{:S(2)}) async-start(), calls=%async_computation.14 | async-start | bytes 2621440 | tf_op jit(solution)/shard_map/all_gather | solution.py:29
  92.3 130.9 %copy-start.62 = (f32[1,1,1024]{2,1,0:T(1,128)}, f32[1,1,1024]{2,1,0:T(1,128)S(1)}, u32[]{:S(2)}) copy-start(f32[1,1,1024]{2,1,0:T(1,128)S(1)} %get-tuple-element.174) | copy-start | bytes 12292
  172.1 106.8 %reduce-scatter.19.cloned.1.call-start = ((), (), s32[]{:S(2)}) async-start(), calls=%async_computation.15 | async-start | bytes 2621440 | tf_op jit(solution)/shard_map/reduce_scatter | solution.py:41
  236.4 91.3 %all-gather.13.cloned.1.call-start = ((), (), s32[]{:S(2)}) async-start(), calls=%async_computation.16 | async-start | bytes 2621440 | tf_op jit(solution)/shard_map/all_gather | solution.py:29
  282.6 152.8 %reduce-scatter.21.cloned.1.call-start = ((), (), s32[]{:S(2)}) async-start(), calls=%async_computation.17 | async-start | bytes 5242880 | tf_op jit(solution)/shard_map/reduce_scatter | solution.py:54
  359.7 126.1 %all-gather.15.cloned.1.call-start = ((), (), s32[]{:S(2)}) async-start(), calls=%async_computation.18 | async-start | bytes 2621440 | tf_op jit(solution)/shard_map/all_gather | solution.py:29
  439.4 106.8 %reduce-scatter.23.cloned.1.call-start = ((), (), s32[]{:S(2)}) async-start(), calls=%async_computation.19 | async-start | bytes 2621440 | tf_op jit(solution)/shard_map/reduce_scatter | solution.py:41
  503.6 93.1 %all-gather.17.cloned.1.call-start = ((), (), s32[]{:S(2)}) async-start(), calls=%async_computation.20 | async-start | bytes 2621440 | tf_op jit(solution)/shard_map/all_gather | solution.py:33
  551.7 108.3 %reduce-scatter.25.cloned.1.call-start = ((), (), s32[]{:S(2)}) async-start(), calls=%async_computation.21 | async-start | bytes 2621440 | tf_op jit(solution)/shard_map/reduce_scatter | solution.py:73
  617.4 94.2 %all-gather.19.cloned.1.call-start = ((), (), s32[]{:S(2)}) async-start(), calls=%async_computation.22 | async-start | bytes 2621440 | tf_op jit(solution)/shard_map/all_gather | solution.py:33
  666.6 141.2 %reduce-scatter.27.cloned.1.call-start = ((), (), s32[]{:S(2)}) async-start(), calls=%async_computation.23 | async-start | bytes 2621440 | tf_op jit(solution)/shard_map/reduce_scatter | solution.py:73
  765.2 93.6 %all-gather.21.cloned.1.call-start = ((), (), s32[]{:S(2)}) async-start(), calls=%async_computation.24 | async-start | bytes 2621440 | tf_op jit(solution)/shard_map/all_gather | solution.py:33
  813.8 108.6 %reduce-scatter.29.cloned.1.call-start = ((), (), s32[]{:S(2)}) async-start(), calls=%async_computation.25 | async-start | bytes 2621440 | tf_op jit(solution)/shard_map/reduce_scatter | solution.py:73
  879.9 94.1 %all-gather.23.cloned.1.call-start = ((), (), s32[]{:S(2)}) async-start(), calls=%async_computation.26 | async-start | bytes 2621440 | tf_op jit(solution)/shard_map/all_gather | solution.py:33
  929.0 150.8 %reduce-scatter.39.cloned.1.call-start = ((), (), s32[]{:S(2)}) async-start(), calls=%async_computation.31 | async-start | bytes 4718592
  956.7 155.3 %reduce-scatter.37.cloned.1.call-start = ((), (), s32[]{:S(2)}) async-start(), calls=%async_computation.30 | async-start | bytes 1179648
  1026.8 87.5 %reduce-scatter.31.cloned.1.call-start = ((), (), s32[]{:S(2)}) async-start(), calls=%async_computation.27 | async-start | bytes 2621440 | tf_op jit(solution)/shard_map/reduce_scatter | solution.py:73
  1042.7 118.9 %reduce-scatter.33.cloned.1.call-start = ((), (), s32[]{:S(2)}) async-start(), calls=%async_computation.28 | async-start | bytes 3538944 | tf_op jit(solution)/shard_map/reduce_scatter | solution.py:319
  1052.1 184.2 %reduce-scatter.35.cloned.1.call-start = ((), (), s32[]{:S(2)}) async-start(), calls=%async_computation.29 | async-start | bytes 9437184 | tf_op jit(solution)/shard_map/reduce_scatter | solution.py:325
  1109.4 130.6 %copy-start.84 = (f32[2,2,1024]{2,1,0:T(2,128)}, f32[2,2,1024]{2,1,0:T(2,128)S(1)}, u32[]{:S(2)}) copy-start(f32[2,2,1024]{2,1,0:T(2,128)S(1)} %get-tuple-element.138) | copy-start | bytes 49156
  1109.4 130.6 %copy-start.109 = (f32[2,256]{1,0:T(2,128)}, f32[2,256]{1,0:T(2,128)S(1)}, u32[]{:S(2)}) copy-start(f32[2,256]{1,0:T(2,128)S(1)} %get-tuple-element.137) | copy-start | bytes 6148
  (137 other events, 2584.4 us)
Sparse Core Ops, SparseCore 0:
  11.1 48.3 all-gather.8
  91.7 75.5 reduce-scatter.16
  172.3 46.1 all-gather.10
  236.5 42.4 reduce-scatter.18
  282.8 44.8 all-gather.12
  359.8 75.5 reduce-scatter.20
  439.6 46.1 all-gather.14
  503.7 42.4 reduce-scatter.22
  551.8 44.8 all-gather.16
  617.5 42.4 reduce-scatter.24
  666.7 44.8 all-gather.18
  765.3 42.4 reduce-scatter.26
  813.9 44.8 all-gather.20
  880.0 42.4 reduce-scatter.28
  929.2 44.8 all-gather.22
  977.2 49.9 reduce-scatter.38
  1030.3 36.0 reduce-scatter.36
  1069.0 43.5 reduce-scatter.30
  1116.1 45.4 reduce-scatter.32
  1164.8 71.4 reduce-scatter.34
where the time goes:
time: 1300 us; the launch traced here: 1290 us
  waiting for transfers between devices  768 us (59%)
  matrix products  238 us (18%)
  other arithmetic  111 us (9%)
  blocking collectives  103 us (8%)
  local copies, waits for them, and re-layouts  46.2 us (4%)
  between operations  23 us (2%)
    all_gather x4, waiting for transfers between devices, spread_rows(): return lax.all_gather(local_values, 'head', axis=0, tiled=True)  179 us
    reduce_scatter x2, waiting for transfers between devices, branch_output(): lax.psum_scatter(partial_term(jnp.int32(0), local_rows * lax.axis_size('h...  151 us
    all_gather x4, waiting for transfers between devices, spread_grads(): return lax.all_gather(local_values, 'head', axis=0, tiled=True)  148 us
    reduce_scatter x4, waiting for transfers between devices, collect_grads(): lax.psum_scatter(partial_term(jnp.int32(0), local_rows * lax.axis_size('h...  128 us
    reduce_scatter x2, waiting for transfers between devices, collect_rows(): lax.psum_scatter(partial_term(jnp.int32(0), local_rows * lax.axis_size('h...  85.1 us
    reduce_scatter x1, waiting for transfers between devices, on_device(): lax.psum_scatter(expand_stack.astype(jnp.bfloat16), 'dp', scatter_dimensi...  70.9 us
    unnamed x290, local copies, waits for them, and re-layouts  40.8 us
    psum x1, blocking collectives, on_device(): total_norm = jnp.sqrt(lax.psum(squares, ('dp', 'head')))  39.2 us
  transfers between devices with their start and end apart: 20, of which 17 were waited for; matrix products, arithmetic and copies ran while one was open for 11% of the time, Pallas kernels for 0%

commit v1 on v0

v1 whole, which is shorter than its diff:
```python
import functools, math
import jax
import jax.numpy as jnp
from jax import lax
from jax.experimental import pallas as pl
from jax.experimental.pallas import tpu as pltpu
from jax.sharding import Mesh
from jax.sharding import PartitionSpec as P

D = 1024
HDIM = 64
BLOCK = 256
DOC_LIMIT = 512
SCALE = HDIM**0.5
EXP2_SCALE = SCALE * math.log2(math.e)
NT = (((1,), (1,)), ((), ()))
TN = (((0,), (0,)), ((), ()))
NN = (((1,), (0,)), ((), ()))


def mm(a, b, dims=NN):
    return lax.dot_general(a, b, dims, preferred_element_type=jnp.float32)


def head_lanes(shape, h):
    lanes = lax.broadcasted_iota(jnp.int32, shape, 1)
    return (lanes >= h * HDIM) & (lanes < (h + 1) * HDIM)


def reach(blocks):
    return min(blocks, -(-(DOC_LIMIT - 1) // BLOCK) + 1)


def by_window(i, blocks, run):
    most = reach(blocks)
    for n in range(1, most + 1):
        test = i == n - 1 if n < most else i >= n - 1
        pl.when(test)(functools.partial(run, n))


def attend_kernel(slot_ref, q_ref, k_ref, v_ref, rows_ref, cols_ref, ctx_ref, stat_ref):
    i = pl.program_id(0)
    width = q_ref.shape[1]

    def run(n):
        q = q_ref[...]
        doc_q = cols_ref[...]
        keys, values, masks = [], [], []
        for o in range(n):
            at = pl.ds(pl.multiple_of(slot_ref[i - o] * BLOCK, BLOCK), BLOCK)
            keys.append(k_ref[at, :])
            values.append(v_ref[at, :])
            doc_k = rows_ref[0:1, pl.ds(pl.multiple_of((i - o) * BLOCK, BLOCK), BLOCK)]
            seen = doc_q == doc_k
            if o == 0:
                shape = (BLOCK, BLOCK)
                seen = seen & (
                    lax.broadcasted_iota(jnp.int32, shape, 1)
                    <= lax.broadcasted_iota(jnp.int32, shape, 0)
                )
            masks.append(jnp.where(seen, 1.0, 0.0))
        context = jnp.zeros((BLOCK, width), jnp.float32)
        stats = jnp.zeros((BLOCK, 128), jnp.float32)
        for h in range(width // HDIM):
            mine = head_lanes((BLOCK, width), h)
            q_h = jnp.where(mine, q, jnp.zeros_like(q))
            total = None
            product = None
            for o in range(n):
                powers = jnp.exp2(mm(q_h, keys[o], NT) * EXP2_SCALE) * masks[o]
                part = jnp.sum(powers, axis=1, keepdims=True)
                term = mm(powers.astype(jnp.bfloat16), values[o])
                total = part if total is None else total + part
                product = term if product is None else product + term
            inverse = 1.0 / total
            context = jnp.where(mine, product * inverse, context)
            stats = jnp.where(
                lax.broadcasted_iota(jnp.int32, (BLOCK, 128), 1) == h, inverse, stats
            )
        ctx_ref[...] = context.astype(jnp.bfloat16)
        stat_ref[...] = stats.T[:8, :]

    by_window(i, k_ref.shape[0] // BLOCK, run)


def attend_forward(slots, q, k, v, rows, cols):
    length, width = q.shape
    blocks = length // BLOCK
    work = reach(blocks) * blocks * (width // HDIM) * 4 * BLOCK * BLOCK * width
    whole = pl.BlockSpec((length, width), lambda i, s: (0, 0))
    return pl.pallas_call(
        attend_kernel,
        out_shape=(
            jax.ShapeDtypeStruct((length, width), jnp.bfloat16),
            jax.ShapeDtypeStruct((8, length), jnp.float32),
        ),
        grid_spec=pltpu.PrefetchScalarGridSpec(
            num_scalar_prefetch=1,
            grid=(blocks,),
            in_specs=[
                pl.BlockSpec((BLOCK, width), lambda i, s: (s[i], 0)),
                whole,
                whole,
                pl.BlockSpec((8, length), lambda i, s: (0, 0)),
                pl.BlockSpec((BLOCK, 1), lambda i, s: (i, 0)),
            ],
            out_specs=[
                pl.BlockSpec((BLOCK, width), lambda i, s: (s[i], 0)),
                pl.BlockSpec((8, BLOCK), lambda i, s: (0, i)),
            ],
        ),
        compiler_params=pltpu.CompilerParams(dimension_semantics=("arbitrary",)),
        cost_estimate=pl.CostEstimate(
            flops=work, bytes_accessed=8 * length * width, transcendentals=0
        ),
    )(slots, q, k, v, rows, cols)


def attend_grad_kernel(
    slot_ref, q_ref, k_ref, v_ref, ctx_ref, grad_ref, rows_ref, cols_ref, stat_ref,
    dq_ref, dk_ref, dv_ref, dk_acc, dv_acc,
):
    i = pl.program_id(0)
    width = q_ref.shape[1]
    heads = width // HDIM

    def run(n):
        q = q_ref[...]
        grad = grad_ref[...]
        both = grad.astype(jnp.float32) * ctx_ref[...].astype(jnp.float32)
        high = both.astype(jnp.bfloat16)
        low = (both - high.astype(jnp.float32)).astype(jnp.bfloat16)
        pick_shape = (8, width)
        pick = jnp.where(
            lax.broadcasted_iota(jnp.int32, pick_shape, 1) // HDIM
            == lax.broadcasted_iota(jnp.int32, pick_shape, 0),
            1.0,
            0.0,
        ).astype(jnp.bfloat16)
        inner = mm(pick, high, NT) + mm(pick, low, NT)
        doc_q = rows_ref[0:1, :]
        spots, keys, values, masks = [], [], [], []
        for o in range(n):
            at = pl.ds(pl.multiple_of(slot_ref[i - o] * BLOCK, BLOCK), BLOCK)
            spots.append(at)
            keys.append(k_ref[at, :])
            values.append(v_ref[at, :])
            doc_k = cols_ref[pl.ds(pl.multiple_of((i - o) * BLOCK, BLOCK), BLOCK), :]
            seen = doc_q == doc_k
            if o == 0:
                shape = (BLOCK, BLOCK)
                seen = seen & (
                    lax.broadcasted_iota(jnp.int32, shape, 0)
                    <= lax.broadcasted_iota(jnp.int32, shape, 1)
                )
            masks.append(jnp.where(seen, 1.0, 0.0))
        dq = jnp.zeros((BLOCK, width), jnp.float32)
        dk = [None] * n
        dv = [None] * n
        for h in range(heads):
            mine = head_lanes((BLOCK, width), h)
            q_h = jnp.where(mine, q, jnp.zeros_like(q))
            grad_h = jnp.where(mine, grad, jnp.zeros_like(grad))
            inverse = stat_ref[h : h + 1, :]
            inner_h = inner[h : h + 1, :]
            dq_h = None
            for o in range(n):
                powers = jnp.exp2(mm(keys[o], q_h, NT) * EXP2_SCALE) * masks[o]
                probs = powers * inverse
                slope = (probs * (mm(values[o], grad_h, NT) - inner_h)).astype(jnp.bfloat16)
                term = mm(probs.astype(jnp.bfloat16), grad_h)
                dv[o] = term if dv[o] is None else dv[o] + term
                term = mm(slope, q_h)
                dk[o] = term if dk[o] is None else dk[o] + term
                term = mm(slope, keys[o], TN)
                dq_h = term if dq_h is None else dq_h + term
            dq = jnp.where(mine, dq_h, dq)
        dq_ref[...] = dq * SCALE
        for o in range(n):
            if o == 0:
                dk_acc[spots[o], :] = dk[o]
                dv_acc[spots[o], :] = dv[o]
            else:
                dk_acc[spots[o], :] += dk[o]
                dv_acc[spots[o], :] += dv[o]

    by_window(i, k_ref.shape[0] // BLOCK, run)

    @pl.when(i == pl.num_programs(0) - 1)
    def _():
        dk_ref[...] = dk_acc[...] * SCALE
        dv_ref[...] = dv_acc[...].astype(jnp.bfloat16)


def attend_backward(slots, q, k, v, ctx, grad, rows, cols, stats):
    length, width = q.shape
    blocks = length // BLOCK
    work = reach(blocks) * blocks * (width // HDIM) * 10 * BLOCK * BLOCK * width
    whole = pl.BlockSpec((length, width), lambda i, s: (0, 0))
    part = pl.BlockSpec((BLOCK, width), lambda i, s: (s[i], 0))
    return pl.pallas_call(
        attend_grad_kernel,
        out_shape=(
            jax.ShapeDtypeStruct((length, width), jnp.float32),
            jax.ShapeDtypeStruct((length, width), jnp.float32),
            jax.ShapeDtypeStruct((length, width), jnp.bfloat16),
        ),
        grid_spec=pltpu.PrefetchScalarGridSpec(
            num_scalar_prefetch=1,
            grid=(blocks,),
            in_specs=[
                part,
                whole,
                whole,
                part,
                part,
                pl.BlockSpec((8, BLOCK), lambda i, s: (0, i)),
                pl.BlockSpec((length, 1), lambda i, s: (0, 0)),
                pl.BlockSpec((8, BLOCK), lambda i, s: (0, i)),
            ],
            out_specs=[part, whole, whole],
            scratch_shapes=[
                pltpu.VMEM((length, width), jnp.float32),
                pltpu.VMEM((length, width), jnp.float32),
            ],
        ),
        compiler_params=pltpu.CompilerParams(dimension_semantics=("arbitrary",)),
        cost_estimate=pl.CostEstimate(
            flops=work, bytes_accessed=20 * length * width, transcendentals=0
        ),
    )(slots, q, k, v, ctx, grad, rows, cols, stats)


def sphere(values):
    return values * lax.rsqrt(jnp.sum(values * values, axis=-1, keepdims=True) + 1e-06)


def blend_unit(hidden, branch, mixing):
    return sphere(hidden + mixing * (sphere(branch) - hidden))


def gated_units(up_part, gate_part, up_gain, gate_gain):
    return up_part * up_gain * jax.nn.silu(gate_part * gate_gain * D**0.5)


def unit_heads(values, scales):
    heads_here = values.shape[1] // HDIM
    split = values.reshape(values.shape[0], heads_here, HDIM)
    return (sphere(split) * scales.reshape(heads_here, HDIM)).reshape(values.shape)


def flip(values, axis):
    return lax.ppermute(values, axis, [(0, 1), (1, 0)])


def trade(values):
    return lax.ppermute(values, ("core", "zh"), [(0, 0), (1, 2), (2, 1), (3, 3)])


def paired():
    return lax.axis_size("zl") == 2


def gather_rows(block):
    if not paired():
        return lax.all_gather(block, ("core", "zl"), axis=0, tiled=True)
    far = flip(block, "zl")
    near = flip(block, "core")
    return jnp.concatenate([block, near, far, flip(far, "core")])


def scatter_rows(product, local_rows):
    if not paired():
        return lax.psum_scatter(
            product.astype(jnp.bfloat16), ("core", "zl"), scatter_dimension=0, tiled=True
        ).astype(jnp.float32)
    own, near, far, cross = [
        product[n * local_rows : (n + 1) * local_rows] for n in range(4)
    ]
    low = jnp.bfloat16
    far_sum = far + flip(cross.astype(low), "core").astype(jnp.float32)
    near_sum = own + flip(near.astype(low), "core").astype(jnp.float32)
    return near_sum + flip(far_sum.astype(low), "zl").astype(jnp.float32)


def block_slots(length, local_rows):
    blocks = jnp.arange(length // BLOCK, dtype=jnp.int32)
    if not paired():
        return blocks
    per_slot = local_rows // BLOCK
    quarter = blocks // per_slot
    core = (quarter // 2) ^ lax.axis_index("core")
    side = (quarter % 2) ^ lax.axis_index("zl")
    return (side * 2 + core) * per_slot + blocks % per_slot


def fetch_weight(piece):
    return lax.all_gather(trade(piece), "xy", axis=0, tiled=True)


def own_part(values, axis, name):
    size = values.shape[axis] // lax.axis_size(name)
    return lax.dynamic_slice_in_dim(values, lax.axis_index(name) * size, size, axis)


def fetch_layer(attend_weight, output_weight, expand_weight, reduce_weight):
    rows = own_part(attend_weight, 1, "xy")
    columns = own_part(output_weight, 1, "xy")
    attend = fetch_weight(jnp.concatenate([rows[0], rows[1], rows[2], columns.T], axis=1))
    rows = own_part(expand_weight, 1, "xy")
    expand = fetch_weight(jnp.concatenate([rows[0], rows[1]], axis=1))
    return (attend, expand, fetch_weight(own_part(reduce_weight, 0, "xy")))


def return_gradient(part):
    piece = lax.psum_scatter(part, "xy", scatter_dimension=0, tiled=True)
    other = lax.ppermute(piece, ("core", "zh"), [(1, 0), (2, 3)])
    total = piece.astype(jnp.float32) + other.astype(jnp.float32)
    half = total.shape[0] // 2
    core = lax.axis_index("core")
    stay = lax.dynamic_slice_in_dim(total, core * half, half)
    leave = lax.dynamic_slice_in_dim(total, (1 - core) * half, half)
    moved = lax.ppermute(leave.astype(jnp.bfloat16), ("core", "zh"), [(0, 2), (3, 1)])
    return jnp.where(core == lax.axis_index("zh"), stay, moved.astype(jnp.float32))


def pair_lists(size):
    steps = []
    width = 1
    while width < size:
        steps.append([(n, n ^ width) for n in range(size)])
        width *= 2
    return steps


def add_over(values, axes):
    for axis in axes:
        for pairs in pair_lists(lax.axis_size(axis)):
            values = values + lax.ppermute(values, axis, pairs)
    return values


def rows_product(rows_low, grads_low):
    return lax.dot_general(rows_low, grads_low, TN, preferred_element_type=jnp.float32).astype(
        jnp.bfloat16
    )


def dot(left, right, dims=NN):
    return lax.dot_general(left, right, dims, preferred_element_type=jnp.float32)


def on_device(
    stream,
    cotangent,
    documents,
    attend_weight,
    output_weight,
    expand_weight,
    reduce_weight,
    score_gain,
    unit_gain,
    alphas,
):
    low = jnp.bfloat16
    local_rows = stream.shape[0]
    depth = attend_weight.shape[0]
    length = documents.shape[1]
    features = attend_weight.shape[3]
    units_here = reduce_weight.shape[1]
    weights = [None] * depth
    hidden = trade(sphere(stream).astype(low)).astype(jnp.float32)
    small = jnp.concatenate(
        [
            documents.reshape(-1).astype(jnp.float32),
            score_gain.reshape(-1),
            unit_gain.reshape(-1),
        ]
    ).reshape(-1, 128)
    small = trade(small).reshape(-1)
    labels = small[: documents.size].reshape(documents.shape)
    score_gain = small[documents.size : documents.size + score_gain.size].reshape(
        score_gain.shape
    )
    unit_gain = small[documents.size + score_gain.size :].reshape(unit_gain.shape)
    doc_rows = jnp.broadcast_to(labels.reshape(1, -1), (8, labels.size))
    doc_columns = labels.reshape(-1, 1)
    slots = block_slots(length, local_rows)
    for layer in range(depth):
        weights[layer] = fetch_layer(
            attend_weight[layer], output_weight[layer], expand_weight[layer], reduce_weight[layer]
        )
    flowing = trade(cotangent.astype(low)).astype(jnp.float32)
    records = []
    for layer in range(depth):
        attend, expand, reduce = weights[layer]
        attend_rows = gather_rows(hidden.astype(low))
        queries = dot(attend_rows, attend[:, :features])
        key_rows = dot(attend_rows, attend[:, features : 2 * features])
        value_rows = dot(attend_rows, attend[:, 2 * features : 3 * features]).astype(low)
        query_unit = unit_heads(queries, score_gain[layer]).astype(low)
        key_unit = unit_heads(key_rows, score_gain[layer]).astype(low)
        context, stats = attend_forward(
            slots, query_unit, key_unit, value_rows, doc_rows, doc_columns
        )
        branch = scatter_rows(dot(context, attend[:, 3 * features :], NT), local_rows)
        middle = blend_unit(hidden, branch, alphas[layer, 0])
        expand_rows = gather_rows(middle.astype(low))
        up_part = dot(expand_rows, expand[:, :units_here])
        gate_part = dot(expand_rows, expand[:, units_here:])
        units = gated_units(up_part, gate_part, unit_gain[layer, 0], unit_gain[layer, 1]).astype(
            low
        )
        reduced = scatter_rows(dot(units, reduce), local_rows)
        records.append(
            (
                hidden,
                middle,
                branch,
                reduced,
                attend_rows,
                expand_rows,
                queries,
                key_rows,
                query_unit,
                key_unit,
                value_rows,
                context,
                stats,
                up_part,
                gate_part,
                units,
            )
        )
        hidden = blend_unit(middle, reduced, alphas[layer, 1])
    result = trade(hidden.astype(low)).astype(jnp.float32)
    weight_parts = [None] * depth
    score_parts = [None] * depth
    unit_parts = [None] * depth
    alpha_parts = [None] * depth
    for layer in range(depth - 1, -1, -1):
        (
            before,
            middle,
            branch,
            reduced,
            attend_rows,
            expand_rows,
            queries,
            key_rows,
            query_unit,
            key_unit,
            value_rows,
            context,
            stats,
            up_part,
            gate_part,
            units,
        ) = records[layer]
        attend, expand, reduce = weights[layer]
        unused, pullback = jax.vjp(blend_unit, middle, reduced, alphas[layer, 1])
        middle_grad, reduced_grad, alpha_second = pullback(flowing)
        reduced_full = gather_rows(reduced_grad.astype(low))
        units_grad = dot(reduced_full, reduce, NT)
        reduce_part = return_gradient(rows_product(reduced_full, units))
        unused, pull_gate = jax.vjp(
            gated_units, up_part, gate_part, unit_gain[layer, 0], unit_gain[layer, 1]
        )
        up_grad, gate_grad, up_gain_grad, gate_gain_grad = pull_gate(units_grad)
        pair_low = jnp.concatenate([up_grad.astype(low), gate_grad.astype(low)], axis=1)
        middle_grad = middle_grad + scatter_rows(dot(pair_low, expand, NT), local_rows)
        expand_part = return_gradient(rows_product(expand_rows, pair_low))
        unused, pullback = jax.vjp(blend_unit, before, branch, alphas[layer, 0])
        hidden_grad, branch_grad, alpha_first = pullback(middle_grad)
        branch_full = gather_rows(branch_grad.astype(low))
        context_grad = dot(branch_full, attend[:, 3 * features :]).astype(low)
        query_unit_grad, key_unit_grad, value_low = attend_backward(
            slots,
            query_unit,
            key_unit,
            value_rows,
            context,
            context_grad,
            doc_rows,
            doc_columns,
            stats,
        )
        unused, pull_query = jax.vjp(unit_heads, queries, score_gain[layer])
        query_grad, query_gain = pull_query(query_unit_grad)
        unused, pull_key = jax.vjp(unit_heads, key_rows, score_gain[layer])
        key_grad, key_gain = pull_key(key_unit_grad)
        triple_low = jnp.concatenate(
            [query_grad.astype(low), key_grad.astype(low), value_low], axis=1
        )
        flowing = hidden_grad + scatter_rows(
            dot(triple_low, attend[:, : 3 * features], NT), local_rows
        )
        attend_part = return_gradient(
            jnp.concatenate(
                [rows_product(attend_rows, triple_low), rows_product(branch_full, context)], axis=1
            )
        )
        weight_parts[layer] = (attend_part, expand_part, reduce_part)
        score_parts[layer] = query_gain + key_gain
        unit_parts[layer] = jnp.stack([up_gain_grad, gate_gain_grad])
        alpha_parts[layer] = jnp.stack([alpha_first, alpha_second])
    unused, pullback = jax.vjp(sphere, stream)
    stream_delta = pullback(trade(flowing.astype(low)).astype(jnp.float32))[0]
    score_parts = jnp.stack(score_parts)
    unit_parts = jnp.stack(unit_parts)
    alpha_parts = jnp.stack(alpha_parts)
    vector = jnp.concatenate(
        [score_parts.reshape(-1), unit_parts.reshape(-1), alpha_parts.reshape(-1)]
    ).reshape(-1, 128)
    vector = add_over(vector, ("xy", "zh"))
    cut = (score_parts.size + unit_parts.size) // 128
    mine = trade(vector[:cut]).reshape(-1)
    alpha_delta = add_over(vector[cut:], ("core", "zl")).reshape(alpha_parts.shape)
    score_delta = mine[: score_parts.size].reshape(score_parts.shape)
    unit_delta = mine[score_parts.size :].reshape(unit_parts.shape)
    attend_delta = jnp.stack(
        [
            jnp.stack(
                [part[0][:, n * features : (n + 1) * features] for n in range(3)]
            )
            for part in weight_parts
        ]
    )
    output_delta = jnp.stack([part[0][:, 3 * features :].T for part in weight_parts])
    expand_delta = jnp.stack(
        [
            jnp.stack([part[1][:, :units_here], part[1][:, units_here:]])
            for part in weight_parts
        ]
    )
    reduce_delta = jnp.stack([part[2].T for part in weight_parts])
    squares = jnp.float32(0.0)
    for part in weight_parts:
        for entry in part:
            squares = squares + jnp.sum(entry * entry)
    rows_of = lax.axis_size("xy") * lax.axis_size("core")
    squares = squares + (
        jnp.sum(score_delta * score_delta) + jnp.sum(unit_delta * unit_delta)
    ) / rows_of
    squares = squares + jnp.sum(alpha_delta * alpha_delta) / (
        rows_of * lax.axis_size("zh") * lax.axis_size("zl")
    )
    squares = add_over(
        jnp.broadcast_to(squares, (8, 128)), ("core", "zl", "zh", "xy")
    )
    total_norm = jnp.sqrt(squares[0, 0])
    alpha_mean = jnp.mean(alphas, axis=-1)
    return (
        result,
        stream_delta,
        attend_delta,
        output_delta,
        expand_delta,
        reduce_delta,
        score_delta,
        unit_delta,
        alpha_delta,
        total_norm,
        alpha_mean,
    )


def solution(mesh):
    dp = ("xy", "core")
    head = ("zh", "zl")
    groups, lines = mesh.devices.shape
    inner = Mesh(
        mesh.devices.reshape(groups // 2, 2, 2, lines // 2), ("xy", "core", "zh", "zl")
    )
    return jax.shard_map(
        on_device,
        mesh=inner,
        in_specs=(
            P(dp + head, None),
            P(dp + head, None),
            P(dp, None),
            P(None, None, None, head),
            P(None, head, None),
            P(None, None, None, head),
            P(None, head, None),
            P(None, head),
            P(None, None, head),
            P(),
        ),
        out_specs=(
            P(dp + head, None),
            P(dp + head, None),
            P(None, None, dp, head),
            P(None, head, dp),
            P(None, None, dp, head),
            P(None, head, dp),
            P(None, head),
            P(None, None, head),
            P(),
            P(),
            P(),
        ),
        check_vma=False,
    )
```

time: 1300 us -> 835 us (0.64)
  waiting for transfers between devices: 768 us -> 326 us
  starting transfers between devices: 3.21 us -> 128 us
  matrix products: 238 us -> 132 us
  blocking collectives: 103 us -> 0 us
  local copies, waits for them, and re-layouts: 46.2 us -> 104 us
  other arithmetic: 111 us -> 67.3 us
  Pallas kernels: 0 us -> 42.9 us
    reduce_scatter x10 -> x6, waiting for transfers between devices: 440 us -> 0.07 us  [return_gradient(): piece = lax.psum_scatter(part, 'xy', scatter_dimension=0, tiled=True)]
    all_gather x8 -> x6, waiting for transfers between devices: 328 us -> 0.01 us  [fetch_weight(): return lax.all_gather(trade(piece), 'xy', axis=0, tiled=True)]
    ppermute x0 -> x82, waiting for transfers between devices: none -> 326 us  [the longest x48 207 us: flip(): return lax.ppermute(values, axis, [(0, 1), (1, 0)])]
    ppermute x0 -> x82, starting transfers between devices: none -> 126 us  [the longest x48 79.6 us: flip(): return lax.ppermute(values, axis, [(0, 1), (1, 0)])]
    dot_general x54 -> x30, matrix products: 238 us -> 132 us  [the longest x22 94.8 us: dot(): lax.dot_general(left, right, dims, preferred_element_type=jnp.float32)]
    psum x3 -> x0, blocking collectives: 103 us -> none  [the longest x1 39.2 us: on_device(): total_norm = jnp.sqrt(lax.psum(squares, ('dp', 'head')))]
    pallas_call x0 -> x4, Pallas kernels: none -> 42.9 us  [the longest x2 28.9 us: attend_backward(): pl.pallas_call(attend_grad_kernel, out_shape=(jax.ShapeDtypeStruct((lengt...]
    slice x3 -> x22, local copies, waits for them, and re-layouts: 0.8 us -> 19.9 us  [the longest x1 5.26 us: on_device(): expand_weight[layer]]
  transfers between devices with their start and end apart: 20 -> 94, of which waited for: 17 -> 39; matrix products, arithmetic and copies ran while one was open for 11% -> 30% of each run, Pallas kernels for 0% -> 5%
where the time goes in v1:
time: 835 us; the launch traced here: 824 us
  waiting for transfers between devices  326 us (39%)
  matrix products  132 us (16%)
  starting transfers between devices  128 us (15%)
  local copies, waits for them, and re-layouts  104 us (12%)
  other arithmetic  67.3 us (8%)
  Pallas kernels  42.9 us (5%)
  between operations  24.6 us (3%)
    ppermute x48, waiting for transfers between devices, flip(): return lax.ppermute(values, axis, [(0, 1), (1, 0)])  207 us
    ppermute x6, waiting for transfers between devices, return_gradient(): other = lax.ppermute(piece, ('core', 'zh'), [(1, 0), (2, 3)])  102 us
    dot_general x22, matrix products, dot(): lax.dot_general(left, right, dims, preferred_element_type=jnp.float32)  94.8 us
    ppermute x48, starting transfers between devices, flip(): return lax.ppermute(values, axis, [(0, 1), (1, 0)])  79.6 us
    dot_general x8, matrix products, rows_product(): lax.dot_general(rows_low, grads_low, TN, preferred_element_type=jnp.float32)  36.9 us
    unnamed x273, local copies, waits for them, and re-layouts  34.3 us
    pallas_call x2, Pallas kernels, attend_backward(): pl.pallas_call(attend_grad_kernel, out_shape=(jax.ShapeDtypeStruct((lengt...  28.9 us
    ppermute x10, waiting for transfers between devices, add_over(): values = values + lax.ppermute(values, axis, pairs)  17.3 us
  transfers between devices with their start and end apart: 94, of which 39 were waited for; matrix products, arithmetic and copies ran while one was open for 30% of the time, Pallas kernels for 5%

profile of v1, /device:TPU:0, one launch (start us, length us, event | category | flops | bytes accessed | tf_op | source)
XLA Modules:
  0.0 824.2 jit_solution(13080531773255127774)
XLA Ops:
  39.2 56.2 %collective-permute-start.1 = (bf16[256,1024]{0,1:T(8,128)(2,1)S(1)}, bf16[256,1024]{0,1:T(8,128)(2,1)S(1)}, u32[]{:S(2)}, u32[]{:S(2)}) collective-permute-start(bf16[256,1024]{0,1:T(8,128)(2,1)S(1)} %collective-permute-done), channel_id=1, source_target_pairs={{0,4},{4,0},{1,5},{5,1},{2,6},{6,2},{3,7},{7,3},{8,12},{12,8},{9,1... | collective-permute-start | bytes 1572872 | tf_op jit(solution)/shard_map/ppermute | solution.py:253
  134.3 13.7 %collective-permute-done.8 = bf16[256,1024]{0,1:T(8,128)(2,1)S(1)} collective-permute-done((bf16[256,1024]{0,1:T(8,128)(2,1)S(1)}, bf16[256,1024]{0,1:T(8,128)(2,1)S(1)}, u32[]{:S(2)}, u32[]{:S(2)}) %collective-permute-start.8) | collective-permute-done | bytes 524320 | tf_op jit(solution)/shard_map/ppermute | solution.py:253
  157.1 12.7 %collective-permute-done.10 = bf16[256,1024]{0,1:T(8,128)(2,1)} collective-permute-done((bf16[256,1024]{0,1:T(8,128)(2,1)S(1)}, bf16[256,1024]{0,1:T(8,128)(2,1)}, u32[]{:S(2)}, u32[]{:S(2)}) %collective-permute-start.10) | collective-permute-done | bytes 524320 | tf_op jit(solution)/shard_map/ppermute | solution.py:253
  178.7 7.6 multiply_convert_fusion.5
  199.8 22.3 %collective-permute-done.16 = bf16[256,1024]{0,1:T(8,128)(2,1)} collective-permute-done((bf16[256,1024]{0,1:T(8,128)(2,1)}, bf16[256,1024]{0,1:T(8,128)(2,1)}, u32[]{:S(2)}, u32[]{:S(2)}) %collective-permute-start.16) | collective-permute-done | bytes 524320 | tf_op jit(solution)/shard_map/ppermute | solution.py:253
  225.6 13.7 %collective-permute-done.18 = bf16[256,1024]{0,1:T(8,128)(2,1)S(1)} collective-permute-done((bf16[256,1024]{0,1:T(8,128)(2,1)S(1)}, bf16[256,1024]{0,1:T(8,128)(2,1)S(1)}, u32[]{:S(2)}, u32[]{:S(2)}) %collective-permute-start.18) | collective-permute-done | bytes 524320 | tf_op jit(solution)/shard_map/ppermute | solution.py:253
  282.9 16.9 %collective-permute-done.23 = bf16[256,1024]{0,1:T(8,128)(2,1)} collective-permute-done((bf16[256,1024]{0,1:T(8,128)(2,1)}, bf16[256,1024]{0,1:T(8,128)(2,1)}, u32[]{:S(2)}, u32[]{:S(2)}) %collective-permute-start.23) | collective-permute-done | bytes 524320 | tf_op jit(solution)/shard_map/ppermute | solution.py:253
  303.9 13.5 %collective-permute-done.25 = bf16[256,1024]{0,1:T(8,128)(2,1)} collective-permute-done((bf16[256,1024]{0,1:T(8,128)(2,1)}, bf16[256,1024]{0,1:T(8,128)(2,1)}, u32[]{:S(2)}, u32[]{:S(2)}) %collective-permute-start.25) | collective-permute-done | bytes 524320 | tf_op jit(solution)/shard_map/ppermute | solution.py:253
  326.4 7.7 multiply_convert_fusion.4
  347.2 15.3 %collective-permute-done.31 = bf16[256,1024]{0,1:T(8,128)(2,1)} collective-permute-done((bf16[256,1024]{0,1:T(8,128)(2,1)}, bf16[256,1024]{0,1:T(8,128)(2,1)}, u32[]{:S(2)}, u32[]{:S(2)}) %collective-permute-start.31) | collective-permute-done | bytes 524320 | tf_op jit(solution)/shard_map/ppermute | solution.py:253
  366.6 13.0 %collective-permute-done.35 = bf16[256,1024]{0,1:T(8,128)(2,1)S(1)} collective-permute-done((bf16[256,1024]{0,1:T(8,128)(2,1)S(1)}, bf16[256,1024]{0,1:T(8,128)(2,1)S(1)}, u32[]{:S(2)}, u32[]{:S(2)}) %collective-permute-start.35) | collective-permute-done | bytes 524320 | tf_op jit(solution)/shard_map/ppermute | solution.py:253
  398.3 13.5 %collective-permute-done.39 = bf16[256,1024]{0,1:T(8,128)(2,1)S(1)} collective-permute-done((bf16[256,1024]{0,1:T(8,128)(2,1)S(1)}, bf16[256,1024]{0,1:T(8,128)(2,1)S(1)}, u32[]{:S(2)}, u32[]{:S(2)}) %collective-permute-start.39) | collective-permute-done | bytes 524320 | tf_op jit(solution)/shard_map/ppermute | solution.py:253
  419.3 8.8 %collective-permute-done.41 = bf16[256,1024]{0,1:T(8,128)(2,1)S(1)} collective-permute-done((bf16[256,1024]{0,1:T(8,128)(2,1)S(1)}, bf16[256,1024]{0,1:T(8,128)(2,1)S(1)}, u32[]{:S(2)}, u32[]{:S(2)}) %collective-permute-start.41) | collective-permute-done | bytes 524320 | tf_op jit(solution)/shard_map/ppermute | solution.py:253
  433.2 14.5 %shard_map.187 = (f32[1024,256]{1,0:T(8,128)}, f32[1024,256]{1,0:T(8,128)}, bf16[1024,256]{1,0:T(8,128)(2,1)}) custom-call(s32[4]{0:T(128)} %fusion.73.slot_ref, bf16[1024,256]{1,0:T(8,128)(2,1)} %get-tuple-element.196.q_ref, bf16[1024,256]{1,0:T(8,128)(2,1)} %get-tuple-element.99.k_ref, bf16[1024,256]{1,0:T(8,128)(2,1)} %convolution_convert_fusion.10.v_ref, ...), custom_call_target="tpu_custom_call" | custom-call | flops 8053063680 | bytes 5242880 | tf_op jit(solution)/shard_map/pallas_call | solution.py:201
  481.2 7.7 convolution_convert_fusion
  499.1 12.8 %collective-permute-done.47 = bf16[256,1024]{0,1:T(8,128)(2,1)S(1)} collective-permute-done((bf16[256,1024]{0,1:T(8,128)(2,1)S(1)}, bf16[256,1024]{0,1:T(8,128)(2,1)S(1)}, u32[]{:S(2)}, u32[]{:S(2)}) %collective-permute-start.47) | collective-permute-done | bytes 524320 | tf_op jit(solution)/shard_map/ppermute | solution.py:253
  530.5 13.5 %collective-permute-done.51 = bf16[256,1024]{0,1:T(8,128)(2,1)S(1)} collective-permute-done((bf16[256,1024]{0,1:T(8,128)(2,1)S(1)}, bf16[256,1024]{0,1:T(8,128)(2,1)S(1)}, u32[]{:S(2)}, u32[]{:S(2)}) %collective-permute-start.51) | collective-permute-done | bytes 524320 | tf_op jit(solution)/shard_map/ppermute | solution.py:253
  550.1 8.8 %collective-permute-done.53 = bf16[256,1024]{0,1:T(8,128)(2,1)S(1)} collective-permute-done((bf16[256,1024]{0,1:T(8,128)(2,1)S(1)}, bf16[256,1024]{0,1:T(8,128)(2,1)S(1)}, u32[]{:S(2)}, u32[]{:S(2)}) %collective-permute-start.53) | collective-permute-done | bytes 524320 | tf_op jit(solution)/shard_map/ppermute | solution.py:253
  563.6 14.3 %shard_map.188 = (f32[1024,256]{1,0:T(8,128)}, f32[1024,256]{1,0:T(8,128)}, bf16[1024,256]{1,0:T(8,128)(2,1)}) custom-call(s32[4]{0:T(128)} %fusion.73.slot_ref, bf16[1024,256]{1,0:T(8,128)(2,1)} %get-tuple-element.198.q_ref, bf16[1024,256]{1,0:T(8,128)(2,1)} %get-tuple-element.111.k_ref, bf16[1024,256]{1,0:T(8,128)(2,1)} %convolution_convert_fusion.11.v_ref, ...), custom_call_target="tpu_custom_call" | custom-call | flops 8053063680 | bytes 5242880 | tf_op jit(solution)/shard_map/pallas_call | solution.py:201
  598.3 9.3 %convolution_convert_fusion.1 = bf16[1024,2048]{1,0:T(8,128)(2,1)} fusion(bf16[1024,1024]{1,0:T(8,128)(2,1)} %copy-done.46, bf16[1024,1024]{1,0:T(8,128)(2,1)} %copy-done.124, bf16[256,1024]{0,1:T(8,128)(2,1)} %collective-permute-done.11, bf16[256,1024]{0,1:T(8,128)(2,1)} %collective-permute-done.10, bf16[256,1024]{0,1:T(8,128)(2,1)} %collective-permute-done.9, ...), kind=kOutput, calls=%fused_computation.25 | convolution fusion | flops 4313841664 | bytes 10485760 | tf_op jit(solution)/shard_map/dot_general | solution.py:344
  610.8 20.2 %collective-permute-done.69 = bf16[256,1024]{0,1:T(8,128)(2,1)S(1)} collective-permute-done((bf16[256,1024]{0,1:T(8,128)(2,1)}, bf16[256,1024]{0,1:T(8,128)(2,1)S(1)}, u32[]{:S(2)}, u32[]{:S(2)}) %collective-permute-start.69) | collective-permute-done | bytes 524320 | tf_op jit(solution)/shard_map/ppermute | solution.py:317
  686.3 49.2 %collective-permute-done.67 = bf16[256,1024]{0,1:T(8,128)(2,1)S(1)} collective-permute-done((bf16[256,1024]{0,1:T(8,128)(2,1)}, bf16[256,1024]{0,1:T(8,128)(2,1)S(1)}, u32[]{:S(2)}, u32[]{:S(2)}) %collective-permute-start.67) | collective-permute-done | bytes 524320 | tf_op jit(solution)/shard_map/ppermute | solution.py:317
  755.7 22.4 %collective-permute-done.59 = bf16[256,1024]{0,1:T(8,128)(2,1)S(1)} collective-permute-done((bf16[256,1024]{0,1:T(8,128)(2,1)}, bf16[256,1024]{0,1:T(8,128)(2,1)S(1)}, u32[]{:S(2)}, u32[]{:S(2)}) %collective-permute-start.59) | collective-permute-done | bytes 524320 | tf_op jit(solution)/shard_map/ppermute | solution.py:317
  779.6 9.7 %collective-permute-done.63 = bf16[256,2048]{1,0:T(8,128)(2,1)S(1)} collective-permute-done((bf16[256,2048]{1,0:T(8,128)(2,1)}, bf16[256,2048]{1,0:T(8,128)(2,1)S(1)}, u32[]{:S(2)}, u32[]{:S(2)}) %collective-permute-start.63) | collective-permute-done | bytes 1048608 | tf_op jit(solution)/shard_map/ppermute | solution.py:317
  (679 shorter events, 402.0 us)
Async XLA Ops:
  7.2 93.1 %all-gather.7.cloned.1.call-start = ((), (), s32[]{:S(2)}) async-start(), calls=%async_computation.6 | async-start | bytes 2621440 | tf_op jit(solution)/shard_map/all_gather | solution.py:298
  14.5 157.6 %all-gather.9.cloned.1.call-start = ((), (), s32[]{:S(2)}) async-start(), calls=%async_computation.7 | async-start | bytes 5242880 | tf_op jit(solution)/shard_map/all_gather | solution.py:298
  21.9 164.4 %all-gather.11.cloned.1.call-start = ((), (), s32[]{:S(2)}) async-start(), calls=%async_computation.8 | async-start | bytes 2621440 | tf_op jit(solution)/shard_map/all_gather | solution.py:298
  24.6 70.8 %collective-permute-start.5 = (f32[44,128]{1,0:T(8,128)S(1)}, f32[44,128]{1,0:T(8,128)S(1)}, u32[]{:S(2)}, u32[]{:S(2)}) collective-permute-start(f32[44,128]{1,0:T(8,128)S(1)} %maximum_bitcast_fusion.5), channel_id=1, source_target_pairs={{0,0},{2,4},{4,2},{6,6},{1,1},{3,5},{5,3},{7,7},{8,8},{10,12},{12,... | collective-permute-start | bytes 67592 | tf_op jit(solution)/shard_map/ppermute | solution.py:257
  25.3 71.2 %collective-permute-start.2 = (bf16[256,1024]{0,1:T(8,128)(2,1)S(1)}, bf16[256,1024]{0,1:T(8,128)(2,1)S(1)}, u32[]{:S(2)}, u32[]{:S(2)}) collective-permute-start(bf16[256,1024]{0,1:T(8,128)(2,1)S(1)} %collective-permute-done), channel_id=1, source_target_pairs={{0,1},{1,0},{2,3},{3,2},{4,5},{5,4},{6,7},{7,6},{8,9},{9,8},{10,11... | collective-permute-start | bytes 1572872 | tf_op jit(solution)/shard_map/ppermute | solution.py:253
  33.3 97.5 %collective-permute-start.13 = (bf16[256,1024]{1,0:T(8,128)(2,1)}, bf16[256,1024]{1,0:T(8,128)(2,1)}, u32[]{:S(2)}, u32[]{:S(2)}) collective-permute-start(bf16[256,1024]{1,0:T(8,128)(2,1)} %dynamic-slice_bitcast_fusion.5), channel_id=1, source_target_pairs={{0,0},{2,4},{4,2},{6,6},{1,1},{3,5},{5,3},{7,7},{8,8},{10,12},{12,... | collective-permute-start | bytes 1572872 | tf_op jit(solution)/shard_map/ppermute | solution.py:257
  39.2 58.7 %collective-permute-start.1 = (bf16[256,1024]{0,1:T(8,128)(2,1)S(1)}, bf16[256,1024]{0,1:T(8,128)(2,1)S(1)}, u32[]{:S(2)}, u32[]{:S(2)}) collective-permute-start(bf16[256,1024]{0,1:T(8,128)(2,1)S(1)} %collective-permute-done), channel_id=1, source_target_pairs={{0,4},{4,0},{1,5},{5,1},{2,6},{6,2},{3,7},{7,3},{8,12},{12,8},{9,1... | collective-permute-start | bytes 1572872 | tf_op jit(solution)/shard_map/ppermute | solution.py:253
  130.8 108.5 %all-gather.13.cloned.1.call-start = ((), (), s32[]{:S(2)}) async-start(), calls=%async_computation.9 | async-start | bytes 2621440 | tf_op jit(solution)/shard_map/all_gather | solution.py:298
  170.7 146.8 %all-gather.15.cloned.1.call-start = ((), (), s32[]{:S(2)}) async-start(), calls=%async_computation.10 | async-start | bytes 5242880 | tf_op jit(solution)/shard_map/all_gather | solution.py:298
  196.7 25.4 %collective-permute-start.16 = (bf16[256,1024]{0,1:T(8,128)(2,1)}, bf16[256,1024]{0,1:T(8,128)(2,1)}, u32[]{:S(2)}, u32[]{:S(2)}) collective-permute-start(bf16[256,1024]{0,1:T(8,128)(2,1)} %fusion.47), channel_id=1, source_target_pairs={{0,1},{1,0},{2,3},{3,2},{4,5},{5,4},{6,7},{7,6},{8,9},{9,8},{10,11... | collective-permute-start | bytes 1572872 | tf_op jit(solution)/shard_map/ppermute | solution.py:253
  199.3 134.7 %all-gather.17.cloned.1.call-start = ((), (), s32[]{:S(2)}) async-start(), calls=%async_computation.11 | async-start | bytes 2621440 | tf_op jit(solution)/shard_map/all_gather | solution.py:298
  282.7 324.9 %reduce-scatter.17.cloned.1.call-start = ((), (), s32[]{:S(2)}) async-start(), calls=%async_computation.17 | async-start | bytes 2621440 | tf_op jit(solution)/shard_map/reduce_scatter | solution.py:316
  419.1 222.7 %reduce-scatter.9.cloned.1.call-start = ((), (), s32[]{:S(2)}) async-start(), calls=%async_computation.13 | async-start | bytes 2621440 | tf_op jit(solution)/shard_map/reduce_scatter | solution.py:316
  473.2 209.4 %reduce-scatter.13.cloned.1.call-start = ((), (), s32[]{:S(2)}) async-start(), calls=%async_computation.15 | async-start | bytes 5242880 | tf_op jit(solution)/shard_map/reduce_scatter | solution.py:316
  489.0 194.9 %reduce-scatter.15.cloned.1.call-start = ((), (), s32[]{:S(2)}) async-start(), calls=%async_computation.16 | async-start | bytes 2621440 | tf_op jit(solution)/shard_map/reduce_scatter | solution.py:316
  550.0 200.8 %reduce-scatter.7.cloned.1.call-start = ((), (), s32[]{:S(2)}) async-start(), calls=%async_computation.12 | async-start | bytes 2621440 | tf_op jit(solution)/shard_map/reduce_scatter | solution.py:316
  598.0 154.3 %reduce-scatter.11.cloned.1.call-start = ((), (), s32[]{:S(2)}) async-start(), calls=%async_computation.14 | async-start | bytes 5242880 | tf_op jit(solution)/shard_map/reduce_scatter | solution.py:316
  607.6 23.4 %collective-permute-start.69 = (bf16[256,1024]{0,1:T(8,128)(2,1)}, bf16[256,1024]{0,1:T(8,128)(2,1)S(1)}, u32[]{:S(2)}, u32[]{:S(2)}) collective-permute-start(bf16[256,1024]{0,1:T(8,128)(2,1)} %reduce-scatter.17.cloned.1.call-done), channel_id=1, source_target_pairs={{2,0},{4,6},{3,1},{5,7},{10,8},{12,14},{11,9},{13,15},{18,16},{20,... | collective-permute-start | bytes 1572872 | tf_op jit(solution)/shard_map/ppermute | solution.py:317
  609.0 26.8 %collective-permute-start.32 = (bf16[256,1024]{0,1:T(8,128)(2,1)}, bf16[256,1024]{0,1:T(8,128)(2,1)S(1)}, u32[]{:S(2)}, u32[]{:S(2)}) collective-permute-start(bf16[256,1024]{0,1:T(8,128)(2,1)} %get-tuple-element.153), channel_id=1, source_target_pairs={{0,0},{2,4},{4,2},{6,6},{1,1},{3,5},{5,3},{7,7},{8,8},{10,12},{12,... | collective-permute-start | bytes 1572872 | tf_op jit(solution)/shard_map/ppermute | solution.py:257
  641.8 30.0 %collective-permute-start.61 = (bf16[256,1024]{0,1:T(8,128)(2,1)}, bf16[256,1024]{0,1:T(8,128)(2,1)S(1)}, u32[]{:S(2)}, u32[]{:S(2)}) collective-permute-start(bf16[256,1024]{0,1:T(8,128)(2,1)} %reduce-scatter.9.cloned.1.call-done), channel_id=1, source_target_pairs={{2,0},{4,6},{3,1},{5,7},{10,8},{12,14},{11,9},{13,15},{18,16},{20,... | collective-permute-start | bytes 1572872 | tf_op jit(solution)/shard_map/ppermute | solution.py:317
  682.6 55.9 %collective-permute-start.65 = (bf16[256,2048]{1,0:T(8,128)(2,1)}, bf16[256,2048]{1,0:T(8,128)(2,1)}, u32[]{:S(2)}, u32[]{:S(2)}) collective-permute-start(bf16[256,2048]{1,0:T(8,128)(2,1)} %reduce-scatter.13.cloned.1.call-done), channel_id=1, source_target_pairs={{2,0},{4,6},{3,1},{5,7},{10,8},{12,14},{11,9},{13,15},{18,16},{20,... | collective-permute-start | bytes 3145736 | tf_op jit(solution)/shard_map/ppermute | solution.py:317
  683.9 51.6 %collective-permute-start.67 = (bf16[256,1024]{0,1:T(8,128)(2,1)}, bf16[256,1024]{0,1:T(8,128)(2,1)S(1)}, u32[]{:S(2)}, u32[]{:S(2)}) collective-permute-start(bf16[256,1024]{0,1:T(8,128)(2,1)} %reduce-scatter.15.cloned.1.call-done), channel_id=1, source_target_pairs={{2,0},{4,6},{3,1},{5,7},{10,8},{12,14},{11,9},{13,15},{18,16},{20,... | collective-permute-start | bytes 1572872 | tf_op jit(solution)/shard_map/ppermute | solution.py:317
  750.8 27.3 %collective-permute-start.59 = (bf16[256,1024]{0,1:T(8,128)(2,1)}, bf16[256,1024]{0,1:T(8,128)(2,1)S(1)}, u32[]{:S(2)}, u32[]{:S(2)}) collective-permute-start(bf16[256,1024]{0,1:T(8,128)(2,1)} %reduce-scatter.7.cloned.1.call-done), channel_id=1, source_target_pairs={{2,0},{4,6},{3,1},{5,7},{10,8},{12,14},{11,9},{13,15},{18,16},{20,... | collective-permute-start | bytes 1572872 | tf_op jit(solution)/shard_map/ppermute | solution.py:317
  752.3 37.1 %collective-permute-start.63 = (bf16[256,2048]{1,0:T(8,128)(2,1)}, bf16[256,2048]{1,0:T(8,128)(2,1)S(1)}, u32[]{:S(2)}, u32[]{:S(2)}) collective-permute-start(bf16[256,2048]{1,0:T(8,128)(2,1)} %reduce-scatter.11.cloned.1.call-done), channel_id=1, source_target_pairs={{2,0},{4,6},{3,1},{5,7},{10,8},{12,14},{11,9},{13,15},{18,16},{20,... | collective-permute-start | bytes 3145736 | tf_op jit(solution)/shard_map/ppermute | solution.py:317
  (197 other events, 1638.0 us)
Sparse Core Ops, SparseCore 0:
  14.6 54.0 all-gather.6
  71.1 52.5 all-gather.8
  130.9 33.9 all-gather.10
  170.8 35.4 all-gather.12
  208.0 66.1 all-gather.14
  282.8 45.6 all-gather.16
  419.3 35.0 reduce-scatter.16
  473.3 34.6 reduce-scatter.8
  511.0 52.5 reduce-scatter.12
  566.4 35.1 reduce-scatter.14
  605.2 35.9 reduce-scatter.6
  644.0 52.9 reduce-scatter.10
